TPU v7x, 32 devices: a whole 2x2x4 slice. The times are simulated.
32 devices in a mesh: dp: 2 (over y), seq: 16 (over z, x, core).
Axes of the slice: x: 2, y: 2, z: 4, core: 2. Of those that a mesh axis runs over, the one named last changes fastest.
Arguments:
- inputs: bfloat16 [2, 2176, 6144], P('dp', 'seq'), may hold values from -6 to 6
- w_project: bfloat16 [6144, 3, 128], P(('dp', 'seq')), may hold values from -0.078125 to 0.078125
- w_output: bfloat16 [6144, 128], P(('dp', 'seq')), may hold values from -0.078125 to 0.078125
- norm_gain: float32 [128], replicated, may hold values from 0.1 to 1.9
- out_grad: bfloat16 [2, 2176, 6144], P('dp', 'seq'), may hold values from -6 to 6
Outputs:
- input_grad: bfloat16 [2, 2176, 6144], P('dp', 'seq')
All inputs are finite; a program needn't handle non-finite values.
Results may differ from a plain program's by a relative error of at most 0.025.
Values may be sent and summed in bfloat16 or wider, within the bound.
A program may use at most 64 MiB of HBM per device.

v0:
```python
import jax
import jax.numpy as jnp
from jax import lax
from jax.sharding import PartitionSpec as P


def contract(left, right, left_dim, right_dim):
    return lax.dot_general(
        left, right, (((left_dim,), (right_dim,)), ((), ())), preferred_element_type=jnp.float32
    )


def other_blocks(local, reverse):
    every = lax.all_gather(local[None].astype(jnp.bfloat16), "seq", axis=0, tiled=True).astype(
        jnp.float32
    )
    own_index = lax.axis_index("seq")
    rank_list = jnp.arange(every.shape[0], dtype=jnp.int32)
    if reverse:
        selected = rank_list > own_index
    else:
        selected = rank_list < own_index
    return jnp.sum(jnp.where(selected[:, None, None], every, 0.0), axis=0)


def per_device(inputs, w_project, w_output, norm_gain, out_grad):
    proj_full, out_full = (
        lax.all_gather(w_project, ("dp", "seq"), axis=0, tiled=True),
        lax.all_gather(w_output, ("dp", "seq"), axis=0, tiled=True),
    )
    width = proj_full.shape[0]
    head = proj_full.shape[2]
    flat_proj = proj_full.reshape(width, 3 * head)
    tokens = inputs[0]
    grads_in = out_grad[0]
    count = tokens.shape[0]
    projected = jnp.dot(tokens, flat_proj, preferred_element_type=jnp.float32).astype(jnp.bfloat16)
    queries = projected[:, :head]
    key_rows = projected[:, head : 2 * head]
    value_rows = projected[:, 2 * head :]
    row_ids = lax.broadcasted_iota(jnp.int32, (count, count), 0)
    col_ids = lax.broadcasted_iota(jnp.int32, (count, count), 1)
    causal = row_ids >= col_ids
    scores = jnp.where(causal, contract(queries, key_rows, 1, 1), 0.0).astype(jnp.bfloat16)
    intra_part = jnp.dot(scores, value_rows, preferred_element_type=jnp.float32)
    local_state = contract(key_rows, value_rows, 0, 0)
    prior_state = other_blocks(local_state, False).astype(jnp.bfloat16)
    attended = intra_part + jnp.dot(queries, prior_state, preferred_element_type=jnp.float32)
    inv_rms = lax.rsqrt(jnp.mean(attended * attended, axis=-1, keepdims=True) + 1e-06)
    head_grad = jnp.dot(grads_in, out_full, preferred_element_type=jnp.float32)
    scaled = norm_gain * head_grad
    attn_grad = inv_rms * scaled - attended * inv_rms**3 * jnp.mean(
        attended * scaled, axis=-1, keepdims=True
    )
    attn_grad = attn_grad.astype(jnp.bfloat16)
    prob_grad = jnp.where(causal, contract(attn_grad, value_rows, 1, 1), 0.0).astype(jnp.bfloat16)
    local_grad = contract(queries, attn_grad, 0, 0)
    later_state = other_blocks(local_grad, True).astype(jnp.bfloat16)
    query_grad = jnp.dot(prob_grad, key_rows, preferred_element_type=jnp.float32) + contract(
        attn_grad, prior_state, 1, 1
    )
    key_grad = contract(prob_grad, queries, 0, 0) + contract(value_rows, later_state, 1, 1)
    value_grad = contract(scores, attn_grad, 0, 0) + jnp.dot(
        key_rows, later_state, preferred_element_type=jnp.float32
    )
    joined = jnp.concatenate([query_grad, key_grad, value_grad], axis=-1).astype(jnp.bfloat16)
    result = contract(joined, flat_proj, 1, 1).astype(jnp.bfloat16)
    return result[None]


def solution(mesh):
    in_specs = (
        P("dp", "seq", None),
        P(("dp", "seq"), None, None),
        P(("dp", "seq"), None),
        P(),
        P("dp", "seq", None),
    )
    out_specs = P("dp", "seq", None)
    return jax.shard_map(
        per_device, mesh=mesh, in_specs=in_specs, out_specs=out_specs, check_vma=False
    )
```

profile of v0, /device:TPU:0, one launch (start us, length us, event | category | flops | bytes accessed | tf_op | source)
XLA Modules:
  0.0 195.9 jit_solution(18106437344810880376)
XLA Ops:
  6.5 0.7 all-gather.7.cloned.1.call-update
  7.3 0.7 all-gather.5.cloned.1.call-update
  8.0 59.8 %all-gather.7.cloned.1.call-done = bf16[6144,128]{1,0:T(8,128)(2,1)} async-done(((bf16[192,128]{1,0:T(8,128)(2,1)}), bf16[6144,128]{1,0:T(8,128)(2,1)}) %all-gather.7.cloned.1.call-update) | async-done | bytes 1572880 | tf_op jit(solution)/shard_map/all_gather | solution.py:29
  67.8 2.5 %fusion.10 = f32[136,128]{1,0:T(8,128)S(1)} fusion(bf16[6144,128]{1,0:T(8,128)(2,1)} %all-gather.7.cloned.1.call-done, bf16[1,136,6144]{2,1,0:T(8,128)(2,1)} %param.9, f32[128]{0:T(128)} %param.8), kind=kOutput, calls=%fused_computation.15 | convolution fusion | flops 213926912 | bytes 3314176 | tf_op jit(solution)/shard_map/dot_general | solution.py:50
  70.3 63.0 %all-gather.5.cloned.1.call-done = bf16[6144,3,128]{2,0,1:T(8,128)(2,1)} async-done(((bf16[192,3,128]{2,0,1:T(8,128)(2,1)}), bf16[6144,3,128]{2,0,1:T(8,128)(2,1)}) %all-gather.5.cloned.1.call-update) | async-done | bytes 4718608 | tf_op jit(solution)/shard_map/all_gather | solution.py:28
  133.3 6.7 %copy.7 = bf16[6144,3,128]{0,2,1:T(8,128)(2,1)} copy(bf16[6144,3,128]{2,0,1:T(8,128)(2,1)} %all-gather.5.cloned.1.call-done) | data formatting | bytes 9437184 | tf_op jit(solution)/shard_map/all_gather | solution.py:28
  140.0 4.0 %fusion.5 = bf16[136,384]{1,0:T(8,128)(2,1)S(1)} fusion(bf16[6144,384]{0,1:T(8,128)(2,1)} %bitcast.32, bf16[1,136,6144]{2,1,0:T(8,128)(2,1)S(1)} %copy-done), kind=kOutput, calls=%fused_computation.6 | convolution fusion | flops 641780736 | bytes 6494208 | tf_op jit(solution)/shard_map/dot_general | solution.py:37
  144.1 0.2 fusion.8
  144.2 0.2 convolution_convert_fusion.2
  144.4 0.1 fusion.26
  144.6 21.0 %all-gather = bf16[2048,128]{1,0:T(8,128)(2,1)S(1)} all-gather(bf16[128,128]{1,0:T(8,128)(2,1)S(1)} %convolution_convert_fusion.2), channel_id=2, replica_groups=mesh['dp'=2,'seq'=16] {'seq'}, dimensions={0}, use_global_device_ids=true | all-gather | bytes 557056 | tf_op jit(solution)/shard_map/all_gather | solution.py:14
  165.6 0.2 fusion.17
  165.8 0.3 multiply_reduce_fusion.1
  166.3 0.2 fusion.9
  166.4 0.1 fusion.29
  166.6 0.2 fusion.34
  166.8 0.2 convolution_convert_fusion.1
  167.0 0.2 fusion.43
  167.3 0.2 fusion.13
  167.5 18.9 %all-gather.1 = bf16[2048,128]{1,0:T(8,128)(2,1)S(1)} all-gather(bf16[128,128]{1,0:T(8,128)(2,1)S(1)} %convolution_convert_fusion.1), channel_id=3, replica_groups=mesh['dp'=2,'seq'=16] {'seq'}, dimensions={0}, use_global_device_ids=true | all-gather | bytes 557056 | tf_op jit(solution)/shard_map/all_gather | solution.py:14
  186.3 0.2 fusion.16
  186.5 0.2 fusion.14
  186.7 0.2 fusion.15
  186.9 2.2 %fusion = bf16[1,136,6144]{2,1,0:T(8,128)(2,1)} fusion(bf16[6144,384]{0,1:T(8,128)(2,1)S(1)} %bitcast.35, bf16[136,128]{1,0:T(8,128)(2,1)S(1)} %fusion.15, bf16[136,128]{1,0:T(8,128)(2,1)S(1)} %fusion.14, bf16[136,128]{1,0:T(8,128)(2,1)S(1)} %fusion.13), kind=kOutput, calls=%fused_computation.1 | convolution fusion | flops 642877440 | bytes 6494208 | tf_op jit(solution)/shard_map/dot_general | solution.py:8
  (13 shorter events, 0.2 us)
Async XLA Ops:
  6.5 133.5 %copy-start = (bf16[1,136,6144]{2,1,0:T(8,128)(2,1)S(1)}, bf16[1,136,6144]{2,1,0:T(8,128)(2,1)}, u32[]{:S(2)}) copy-start(bf16[1,136,6144]{2,1,0:T(8,128)(2,1)} %param.5) | copy-start | bytes 5013508
  6.5 61.3 %all-gather.7.cloned.1.call-start = ((), (), s32[]{:S(2)}) async-start(), calls=%async_computation.1 | async-start | bytes 1622016 | tf_op jit(solution)/shard_map/all_gather | solution.py:29
  7.3 126.1 %all-gather.5.cloned.1.call-start = ((), (), s32[]{:S(2)}) async-start(), calls=%async_computation | async-start | bytes 4866048 | tf_op jit(solution)/shard_map/all_gather | solution.py:28
  140.0 46.8 %slice-start = ((s8[4718592]{0:T(1024)(128)(4,1)}), s8[4194304]{0:T(1024)(128)(4,1)S(1)}, s32[]{:S(2)}) async-start(s8[4718592]{0:T(1024)(128)(4,1)} %bitcast.33), calls=%async_computation.2 | async-start | bytes 8388608
  140.0 46.8 %slice-start.1 = ((s8[4718592]{0:T(1024)(128)(4,1)}), s8[524288]{0:T(1024)(128)(4,1)S(1)}, s32[]{:S(2)}) async-start(s8[4718592]{0:T(1024)(128)(4,1)} %bitcast.33), calls=%async_computation.3 | async-start | bytes 1048576
Sparse Core Ops, SparseCore 0:
  10.2 57.5 all-gather.6
  70.8 62.5 all-gather.4
where the time goes:
time: 196 us
  waiting for transfers between devices  124 us (63%)
  blocking collectives  39.9 us (20%)
  between operations  13.5 us (7%)
  matrix products  11.1 us (6%)
  local copies, waits for them, and re-layouts  6.7 us (3%)
    all_gather x1, waiting for transfers between devices, per_device(): lax.all_gather(w_project, ('dp', 'seq'), axis=0, tiled=True)  63 us
    all_gather x1, waiting for transfers between devices, per_device(): lax.all_gather(w_output, ('dp', 'seq'), axis=0, tiled=True)  59.8 us
    all_gather x2, blocking collectives, other_blocks(): lax.all_gather(local[None].astype(jnp.bfloat16), 'seq', axis=0, tiled=True)  39.9 us
    all_gather x1, local copies, waits for them, and re-layouts, per_device(): lax.all_gather(w_project, ('dp', 'seq'), axis=0, tiled=True)  6.69 us
    dot_general x1, matrix products, per_device(): jnp.dot(tokens, flat_proj, preferred_element_type=jnp.float32)  4.02 us
  transfers between devices with their start and end apart: 2, of which 2 were waited for; matrix products, arithmetic and copies ran while one was open for 1% of the time, Pallas kernels for 0%

commit v1 on v0

--- a/solution.py
+++ b/solution.py
@@ -1,6 +1,10 @@
+import functools
+
 import jax
 import jax.numpy as jnp
 from jax import lax
+from jax.experimental import pallas as pl
+from jax.experimental.pallas import tpu as pltpu
 from jax.sharding import PartitionSpec as P
 
 
@@ -23,7 +27,7 @@
     return jnp.sum(jnp.where(selected[:, None, None], every, 0.0), axis=0)
 
 
-def per_device(inputs, w_project, w_output, norm_gain, out_grad):
+def per_device_plain(inputs, w_project, w_output, norm_gain, out_grad):
     proj_full, out_full = (
         lax.all_gather(w_project, ("dp", "seq"), axis=0, tiled=True),
         lax.all_gather(w_output, ("dp", "seq"), axis=0, tiled=True),
@@ -68,6 +72,359 @@
     return result[None]
 
 
+CORES = 2
+WIDE = 2
+PIECES = 2
+MESH = pl.DeviceIdType.MESH
+
+
+def fused_kernel(
+    planes, x_hbm, g_hbm, w_hbm, gain_ref, out_hbm,
+    xv, gv, wbuf, ob, st_send, st_in, sum_send, sum_in, acc,
+    load_sem, own_sem, out_sem, recv_sem, send_sem, st_rs, st_ss, sum_rs, sum_ss,
+):
+    y = lax.axis_index("dp")
+    seq = lax.axis_index("seq")
+    core = seq % CORES
+    x = (seq // CORES) % WIDE
+    z = seq // (CORES * WIDE)
+    head = st_send.shape[-1]
+    count, width = xv.shape
+    devices = wbuf.shape[1]
+    rows = wbuf.shape[2]
+    ya, xa = (y + core) % 2, (x + 1 - core) % 2
+    yb, xb = (y + 1 - core) % 2, (x + core) % 2
+
+    def dev(yy, zz, xx, cc):
+        return (yy, (zz * WIDE + xx) * CORES + cc)
+
+    def chip(yy, zz, xx):
+        return (yy * planes + zz) * WIDE + xx
+
+    x_load = pltpu.make_async_copy(x_hbm, xv, load_sem.at[0])
+    g_load = pltpu.make_async_copy(g_hbm, gv, load_sem.at[1])
+    me = chip(y, z, x) * CORES + core
+    own = [
+        pltpu.make_async_copy(w_hbm.at[p], wbuf.at[p, me], own_sem.at[p]) for p in range(PIECES)
+    ]
+    for copy in own:
+        copy.start()
+    x_load.start()
+    g_load.start()
+
+    barrier = pltpu.get_barrier_semaphore()
+    near = [
+        dev(y, z, x, 1 - core),
+        dev(y, z, 1 - x, core),
+        dev(y, z, 1 - x, 1 - core),
+        dev(1 - y, z, x, core),
+    ] + [dev(y, (z + dz) % planes, x, core) for dz in range(1, planes)]
+    for other in near:
+        pl.semaphore_signal(barrier, inc=1, device_id=other, device_id_type=MESH)
+    pl.semaphore_wait(barrier, len(near))
+
+    def shard_copy(way, p, origin, target):
+        slot = wbuf.at[p, origin * CORES + core]
+        kind = 1 if way == 4 else 0
+        return pltpu.make_async_remote_copy(
+            src_ref=slot,
+            dst_ref=slot,
+            send_sem=send_sem.at[way, p, origin],
+            recv_sem=recv_sem.at[kind, p, origin],
+            device_id=target,
+            device_id_type=MESH,
+        )
+
+    targets = [
+        dev(ya, z, xa, core),
+        dev(y, lax.rem(z + 1, planes), x, core),
+        dev(y, lax.rem(z + planes - 1, planes), x, core),
+        dev(yb, z, xb, core),
+        dev(y, z, x, 1 - core),
+    ]
+    sent = []
+
+    def send(way, p, origin, cond=None):
+        copy = shard_copy(way, p, origin, targets[way])
+        sent.append((copy, cond))
+        if cond is None:
+            copy.start()
+        else:
+            pl.when(cond)(copy.start)
+
+    def arrive(p, origin):
+        shard_copy(0, p, origin, targets[0]).wait_recv()
+
+    up, down = z < planes - 1, z > 0
+    lines = [(y, x), (ya, xa)]
+    far_lines = [(yb, xb), (1 - y, 1 - x)]
+
+    def step(p, k):
+        if k == 0:
+            own[p].wait()
+            mine = chip(y, z, x)
+            for way, cond in ((1, up), (2, down), (0, None), (3, None), (4, None)):
+                send(way, p, mine, cond)
+            other = chip(ya, z, xa)
+            arrive(p, other)
+            for way, cond in ((1, up), (2, down), (3, None), (4, None)):
+                send(way, p, other, cond)
+            return
+        for yy, xx in lines:
+            for sign, way in ((-1, 1), (1, 2)):
+                zz = z + sign * k
+                valid = (zz >= 0) if sign < 0 else (zz < planes)
+                onward = jnp.logical_and(valid, up if way == 1 else down)
+                origin = chip(yy, zz, xx)
+                pl.when(valid)(functools.partial(arrive, p, origin))
+                send(way, p, origin, onward)
+                send(3, p, origin, valid)
+                send(4, p, origin, valid)
+
+    def across(p, k):
+        for yy, xx in far_lines:
+            for sign in (-1, 1) if k else (0,):
+                zz = z + sign * k
+                valid = jnp.logical_and(zz >= 0, zz < planes)
+                origin = chip(yy, zz, xx)
+                pl.when(valid)(functools.partial(arrive, p, origin))
+                send(4, p, origin, valid)
+
+    def from_core(p):
+        for origin in range(devices // CORES):
+            pltpu.make_async_remote_copy(
+                src_ref=wbuf.at[p, origin * CORES + 1 - core],
+                dst_ref=wbuf.at[p, origin * CORES + 1 - core],
+                send_sem=send_sem.at[4, p, origin],
+                recv_sem=recv_sem.at[1, p, origin],
+                device_id=targets[4],
+                device_id_type=MESH,
+            ).wait_recv()
+
+    parts = 4 if devices % 4 == 0 else 1
+    group = devices // parts
+    span = group * rows
+
+    def weights(p, i, low, high):
+        block = wbuf[p, i * group : (i + 1) * group]
+        return block.reshape(span, 2 * head)[:, low:high]
+
+    def project(ref, p, low, high):
+        total = None
+        for i in range(parts):
+            term = jnp.dot(
+                ref[:, i * span : (i + 1) * span],
+                weights(p, i, low, high),
+                preferred_element_type=jnp.float32,
+            )
+            total = term if total is None else total + term
+        return total
+
+    place = x * CORES + core
+    state_waits = []
+
+    def plane_peer(j):
+        return (x + j // 2) % 2, (core + j % 2) % 2
+
+    def spread(e, local):
+        st_send[e] = local.astype(jnp.bfloat16)
+        for j in range(1, 4):
+            px, pc = plane_peer(j)
+            copy = pltpu.make_async_remote_copy(
+                src_ref=st_send.at[e],
+                dst_ref=st_in.at[e, place],
+                send_sem=st_ss.at[e, j],
+                recv_sem=st_rs.at[e, place],
+                device_id=dev(y, z, px, pc),
+                device_id_type=MESH,
+            )
+            copy.start()
+            state_waits.append((copy, None))
+
+    def plane_sum(e, local):
+        total = local
+        partial = jnp.zeros_like(local)
+        for j in range(1, 4):
+            px, pc = plane_peer(j)
+            index = px * CORES + pc
+            pltpu.make_async_remote_copy(
+                src_ref=st_send.at[e],
+                dst_ref=st_in.at[e, index],
+                send_sem=st_ss.at[e, j],
+                recv_sem=st_rs.at[e, index],
+                device_id=dev(y, z, px, pc),
+                device_id_type=MESH,
+            ).wait_recv()
+            block = st_in[e, index].astype(jnp.float32)
+            total = total + block
+            chosen = (index < place) if e == 0 else (index > place)
+            partial = partial + jnp.where(chosen, block, 0.0)
+        acc[...] = partial
+        sum_send[e] = total.astype(jnp.bfloat16)
+        for dz in range(1, planes):
+            zz = z + dz if e == 0 else z - dz
+            valid = (zz < planes) if e == 0 else (zz >= 0)
+            copy = pltpu.make_async_remote_copy(
+                src_ref=sum_send.at[e],
+                dst_ref=sum_in.at[e, dz - 1],
+                send_sem=sum_ss.at[e, dz - 1],
+                recv_sem=sum_rs.at[e, dz - 1],
+                device_id=dev(y, zz, x, core),
+                device_id_type=MESH,
+            )
+            pl.when(valid)(copy.start)
+            state_waits.append((copy, valid))
+
+    def collect(e):
+        for dz in range(1, planes):
+            valid = (z - dz >= 0) if e == 0 else (z + dz < planes)
+
+            @pl.when(valid)
+            def _():
+                pltpu.make_async_remote_copy(
+                    src_ref=sum_send.at[e],
+                    dst_ref=sum_in.at[e, dz - 1],
+                    send_sem=sum_ss.at[e, dz - 1],
+                    recv_sem=sum_rs.at[e, dz - 1],
+                    device_id=targets[4],
+                    device_id_type=MESH,
+                ).wait_recv()
+                acc[...] += sum_in[e, dz - 1].astype(jnp.float32)
+
+        return acc[...].astype(jnp.bfloat16)
+
+    for k in range(planes):
+        step(0, k)
+        if k >= 1:
+            across(0, k - 1)
+            step(1, k - 1)
+        if k >= 2:
+            across(1, k - 2)
+    across(0, planes - 1)
+    step(1, planes - 1)
+    if planes >= 2:
+        across(1, planes - 2)
+    from_core(0)
+
+    x_load.wait()
+    kv = project(xv, 0, 0, 2 * head).astype(jnp.bfloat16)
+    key_rows, value_rows = kv[:, :head], kv[:, head:]
+    local_state = contract(key_rows, value_rows, 0, 0)
+    spread(0, local_state)
+    across(1, planes - 1)
+    plane_sum(0, local_state)
+    from_core(1)
+
+    queries = project(xv, 1, 0, head).astype(jnp.bfloat16)
+    g_load.wait()
+    head_grad = project(gv, 1, head, 2 * head)
+    row_ids = lax.broadcasted_iota(jnp.int32, (count, count), 0)
+    col_ids = lax.broadcasted_iota(jnp.int32, (count, count), 1)
+    causal = row_ids >= col_ids
+    scores = jnp.where(causal, contract(queries, key_rows, 1, 1), 0.0).astype(jnp.bfloat16)
+    intra_part = jnp.dot(scores, value_rows, preferred_element_type=jnp.float32)
+    scaled = gain_ref[...] * head_grad
+    prior_state = collect(0)
+    attended = intra_part + jnp.dot(queries, prior_state, preferred_element_type=jnp.float32)
+    inv_rms = lax.rsqrt(jnp.mean(attended * attended, axis=-1, keepdims=True) + 1e-06)
+    attn_grad = inv_rms * scaled - attended * (inv_rms * inv_rms * inv_rms) * jnp.mean(
+        attended * scaled, axis=-1, keepdims=True
+    )
+    attn_grad = attn_grad.astype(jnp.bfloat16)
+    local_grad = contract(queries, attn_grad, 0, 0)
+    spread(1, local_grad)
+    prob_grad = jnp.where(causal, contract(attn_grad, value_rows, 1, 1), 0.0).astype(jnp.bfloat16)
+    query_grad = jnp.dot(prob_grad, key_rows, preferred_element_type=jnp.float32) + contract(
+        attn_grad, prior_state, 1, 1
+    )
+    query_grad = query_grad.astype(jnp.bfloat16)
+    plane_sum(1, local_grad)
+    key_part = contract(prob_grad, queries, 0, 0)
+    value_part = contract(scores, attn_grad, 0, 0)
+    later_state = collect(1)
+    key_grad = key_part + contract(value_rows, later_state, 1, 1)
+    value_grad = value_part + jnp.dot(key_rows, later_state, preferred_element_type=jnp.float32)
+    joined = jnp.concatenate([key_grad, value_grad], axis=-1).astype(jnp.bfloat16)
+    outs = []
+    for i in range(parts):
+        cols = pl.ds(i * span, span)
+        ob[:, i * span : (i + 1) * span] = (
+            contract(joined, weights(0, i, 0, 2 * head), 1, 1)
+            + contract(query_grad, weights(1, i, 0, head), 1, 1)
+        ).astype(jnp.bfloat16)
+        copy = pltpu.make_async_copy(ob.at[:, cols], out_hbm.at[:, cols], out_sem.at[i])
+        copy.start()
+        outs.append(copy)
+    for copy, cond in sent + state_waits:
+        if cond is None:
+            copy.wait_send()
+        else:
+            pl.when(cond)(copy.wait_send)
+    for copy in outs:
+        copy.wait()
+
+
+def per_device_fused(devices, planes, inputs, w_project, w_output, norm_gain, out_grad):
+    tokens, grads_in = inputs[0], out_grad[0]
+    count, width = tokens.shape
+    rows, _, head = w_project.shape
+    keyval = w_project[:, 1:, :].reshape(rows, 2 * head)
+    other = jnp.concatenate([w_project[:, 0, :], w_output], axis=-1)
+    packed = jnp.stack([keyval, other])
+    bf16, f32 = jnp.bfloat16, jnp.float32
+    chips = devices // CORES
+    hops = max(planes - 1, 1)
+    dma = pltpu.SemaphoreType.DMA
+    any_spec = pl.BlockSpec(memory_space=pl.ANY)
+    result = pl.pallas_call(
+        functools.partial(fused_kernel, planes),
+        out_shape=jax.ShapeDtypeStruct((count, width), bf16),
+        in_specs=[any_spec, any_spec, any_spec, pl.BlockSpec(memory_space=pltpu.VMEM)],
+        out_specs=any_spec,
+        scratch_shapes=[
+            pltpu.VMEM((count, width), bf16),
+            pltpu.VMEM((count, width), bf16),
+            pltpu.VMEM((PIECES, devices, rows, 2 * head), bf16),
+            pltpu.VMEM((count, width), bf16),
+            pltpu.VMEM((2, head, head), bf16),
+            pltpu.VMEM((2, 4, head, head), bf16),
+            pltpu.VMEM((2, head, head), bf16),
+            pltpu.VMEM((2, hops, head, head), bf16),
+            pltpu.VMEM((head, head), f32),
+            dma((2,)),
+            dma((PIECES,)),
+            dma((4,)),
+            dma((2, PIECES, chips)),
+            dma((5, PIECES, chips)),
+            dma((2, 4)),
+            dma((2, 4)),
+            dma((2, hops)),
+            dma((2, hops)),
+        ],
+        compiler_params=pltpu.CompilerParams(
+            collective_id=0, has_side_effects=True, vmem_limit_bytes=48 * 1024 * 1024
+        ),
+    )(tokens, grads_in, packed, norm_gain.reshape(1, head))
+    return result[None]
+
+
+def per_device(ndp, nseq, inputs, w_project, w_output, norm_gain, out_grad):
+    rows, head = w_project.shape[0], w_project.shape[2]
+    fits = (
+        ndp == 2
+        and nseq % (CORES * WIDE) == 0
+        and inputs.shape[0] == 1
+        and rows % 16 == 0
+        and (ndp * nseq // 4 * rows) % 128 == 0
+        and head % 128 == 0
+    )
+    if not fits:
+        return per_device_plain(inputs, w_project, w_output, norm_gain, out_grad)
+    return per_device_fused(
+        ndp * nseq, nseq // (CORES * WIDE), inputs, w_project, w_output, norm_gain, out_grad
+    )
+
+
 def solution(mesh):
     in_specs = (
         P("dp", "seq", None),
@@ -78,5 +435,6 @@
     )
     out_specs = P("dp", "seq", None)
     return jax.shard_map(
-        per_device, mesh=mesh, in_specs=in_specs, out_specs=out_specs, check_vma=False
-    )
+        functools.partial(per_device, mesh.shape["dp"], mesh.shape["seq"]),
+        mesh=mesh, in_specs=in_specs, out_specs=out_specs, check_vma=False
+    )

time: 196 us -> 66.4 us (0.34)
  waiting for transfers between devices: 124 us -> 0 us
  Pallas kernels: 0 us -> 58.6 us
  blocking collectives: 39.9 us -> 0 us
  between operations: 13.5 us -> 0.04 us
  matrix products: 11.1 us -> 0 us
    all_gather x2 -> x0, waiting for transfers between devices: 123 us -> none  [the longest x1 63 us: per_device(): lax.all_gather(w_project, ('dp', 'seq'), axis=0, tiled=True)]
    pallas_call x0 -> x1, Pallas kernels: none -> 58.6 us  [per_device_fused(): pl.pallas_call(functools.partial(fused_kernel, planes), out_shape=jax.Sha...]
    all_gather x2 -> x0, blocking collectives: 39.9 us -> none  [other_blocks(): lax.all_gather(local[None].astype(jnp.bfloat16), 'seq', axis=0, tiled=True)]
    dot_general x15 -> x0, matrix products: 11.1 us -> none  [the longest x1 4.02 us: per_device(): jnp.dot(tokens, flat_proj, preferred_element_type=jnp.float32)]
    all_gather x1 -> x0, local copies, waits for them, and re-layouts: 6.69 us -> none  [per_device(): lax.all_gather(w_project, ('dp', 'seq'), axis=0, tiled=True)]
    unnamed x6 -> x7, local copies, waits for them, and re-layouts: 0.01 us -> 4.71 us
  transfers between devices with their start and end apart: 2 -> 0, of which waited for: 2 -> 0; matrix products, arithmetic and copies ran while one was open for 1% -> 0% of each run, Pallas kernels for 0% -> 0%
where the time goes in v1:
time: 66.4 us; the launch traced here: 66.1 us
  Pallas kernels  58.6 us (88%)
  local copies, waits for them, and re-layouts  6.59 us (10%)
  other arithmetic  0.83 us (1%)
    pallas_call x1, Pallas kernels, per_device_fused(): pl.pallas_call(functools.partial(fused_kernel, planes), out_shape=jax.Sha...  58.6 us
    unnamed x7, local copies, waits for them, and re-layouts  4.71 us

profile of v1, /device:TPU:0, one launch (start us, length us, event | category | flops | bytes accessed | tf_op | source)
XLA Modules:
  0.0 66.1 jit_solution(9269316397897484550)
XLA Ops:
  0.0 0.8 %slice_bitcast_fusion = bf16[192,128]{1,0:T(8,128)(2,1)S(1)} fusion(bf16[192,3,128]{2,0,1:T(8,128)(2,1)} %param.6), kind=kLoop, calls=%fused_computation.2 | loop fusion | bytes 98304 | tf_op jit(solution)/shard_map/squeeze | solution.py:372
  0.8 0.8 %maximum_bitcast_fusion = bf16[1,192,256]{2,1,0:T(8,128)(2,1)S(1)} fusion(bf16[192,128]{1,0:T(8,128)(2,1)} %param.7, bf16[192,128]{1,0:T(8,128)(2,1)S(1)} %slice_bitcast_fusion), kind=kLoop, calls=%fused_computation.1 | loop fusion | flops 196608 | bytes 196608 | tf_op jit(solution)/shard_map/stack | solution.py:373
  1.6 0.9 %slice.6 = bf16[192,2,128]{2,0,1:T(8,128)(2,1)S(1)} slice(bf16[192,3,128]{2,0,1:T(8,128)(2,1)} %param.6), slice={[0:192], [1:3], [0:128]} | slice | bytes 196608 | tf_op jit(solution)/shard_map/slice | solution.py:371
  2.5 0.1 copy.6
  2.6 0.1 stack_reshape.3
  2.7 0.0 copy-start
  2.7 1.4 %copy-done = bf16[1,136,6144]{2,1,0:T(8,128)(2,1)S(1)} copy-done((bf16[1,136,6144]{2,1,0:T(8,128)(2,1)S(1)}, bf16[1,136,6144]{2,1,0:T(8,128)(2,1)}, u32[]{:S(2)}) %copy-start) | copy-done | bytes 1671192
  4.2 0.0 copy-start.1
  4.2 1.4 %copy-done.1 = bf16[1,136,6144]{2,1,0:T(8,128)(2,1)S(1)} copy-done((bf16[1,136,6144]{2,1,0:T(8,128)(2,1)S(1)}, bf16[1,136,6144]{2,1,0:T(8,128)(2,1)}, u32[]{:S(2)}) %copy-start.1) | copy-done | bytes 1671192
  5.6 0.0 copy-start.2
  5.6 0.7 copy-done.2
  6.3 58.6 %shard_map.55 = bf16[136,6144]{1,0:T(8,128)(2,1)S(1)} custom-call(bf16[136,6144]{1,0:T(8,128)(2,1)S(1)} %bitcast.9, bf16[136,6144]{1,0:T(8,128)(2,1)S(1)} %bitcast.10, bf16[2,192,256]{2,1,0:T(8,128)(2,1)S(1)} %pad_maximum_fusion.w_hbm, f32[1,128]{1,0:T(1,128)S(1)} %bitcast.11), custom_call_target="tpu_custom_call" | custom-call | tf_op jit(solution)/shard_map/pallas_call | solution.py:379
  64.9 1.2 %copy.8 = bf16[1,136,6144]{2,1,0:T(8,128)(2,1)} copy(bf16[1,136,6144]{2,1,0:T(8,128)(2,1)S(1)} %bitcast.8) | data formatting | bytes 3342336
  (1 shorter events, 0.0 us)
Async XLA Ops:
  2.7 1.4 %copy-start = (bf16[1,136,6144]{2,1,0:T(8,128)(2,1)S(1)}, bf16[1,136,6144]{2,1,0:T(8,128)(2,1)}, u32[]{:S(2)}) copy-start(bf16[1,136,6144]{2,1,0:T(8,128)(2,1)} %param.5) | copy-start | bytes 5013508
  4.2 1.4 %copy-start.1 = (bf16[1,136,6144]{2,1,0:T(8,128)(2,1)S(1)}, bf16[1,136,6144]{2,1,0:T(8,128)(2,1)}, u32[]{:S(2)}) copy-start(bf16[1,136,6144]{2,1,0:T(8,128)(2,1)} %param.9) | copy-start | bytes 5013508
  5.6 0.7 copy-start.2

commit v2 on v1

--- a/solution.py
+++ b/solution.py
@@ -76,11 +76,12 @@
 WIDE = 2
 PIECES = 2
 MESH = pl.DeviceIdType.MESH
+FIRST, UP, DOWN, LAST, CORE = range(5)
 
 
 def fused_kernel(
-    planes, x_hbm, g_hbm, w_hbm, gain_ref, out_hbm,
-    xv, gv, wbuf, ob, st_send, st_in, sum_send, sum_in, acc,
+    planes, x_hbm, g_hbm, w_hbm, o_hbm, gain_ref, out_hbm,
+    xv, gv, wbuf, ob, proj, query_out, st_send, st_in, sum_send, sum_in, acc,
     load_sem, own_sem, out_sem, recv_sem, send_sem, st_rs, st_ss, sum_rs, sum_ss,
 ):
     y = lax.axis_index("dp")
@@ -105,10 +106,22 @@
     g_load = pltpu.make_async_copy(g_hbm, gv, load_sem.at[1])
     me = chip(y, z, x) * CORES + core
     own = [
-        pltpu.make_async_copy(w_hbm.at[p], wbuf.at[p, me], own_sem.at[p]) for p in range(PIECES)
+        [
+            pltpu.make_async_copy(
+                w_hbm.at[1 + j], wbuf.at[0, me, :, pl.ds(j * head, head)], own_sem.at[3 * j]
+            )
+            for j in range(2)
+        ],
+        [
+            pltpu.make_async_copy(
+                w_hbm.at[0], wbuf.at[1, me, :, pl.ds(0, head)], own_sem.at[1]
+            ),
+            pltpu.make_async_copy(o_hbm, wbuf.at[1, me, :, pl.ds(head, head)], own_sem.at[2]),
+        ],
     ]
-    for copy in own:
-        copy.start()
+    for copies in own:
+        for copy in copies:
+            copy.start()
     x_load.start()
     g_load.start()
 
@@ -123,14 +136,16 @@
         pl.semaphore_signal(barrier, inc=1, device_id=other, device_id_type=MESH)
     pl.semaphore_wait(barrier, len(near))
 
-    def shard_copy(way, p, origin, target):
-        slot = wbuf.at[p, origin * CORES + core]
-        kind = 1 if way == 4 else 0
+    cut = rows * 2 // 3 // 16 * 16
+    spans = (pl.ds(0, cut), pl.ds(cut, rows - cut))
+
+    def shard_copy(way, p, part, origin, owner, target):
+        slot = wbuf.at[p, origin * CORES + owner, spans[part]]
         return pltpu.make_async_remote_copy(
             src_ref=slot,
             dst_ref=slot,
-            send_sem=send_sem.at[way, p, origin],
-            recv_sem=recv_sem.at[kind, p, origin],
+            send_sem=send_sem.at[way, p, part, origin],
+            recv_sem=recv_sem.at[1 if way == CORE else 0, p, part, origin],
             device_id=target,
             device_id_type=MESH,
         )
@@ -144,62 +159,121 @@
     ]
     sent = []
 
-    def send(way, p, origin, cond=None):
-        copy = shard_copy(way, p, origin, targets[way])
+    def send(way, p, part, origin, cond=None):
+        copy = shard_copy(way, p, part, origin, core, targets[way])
         sent.append((copy, cond))
         if cond is None:
             copy.start()
         else:
             pl.when(cond)(copy.start)
 
-    def arrive(p, origin):
-        shard_copy(0, p, origin, targets[0]).wait_recv()
+    def arrive(p, part, origin, valid=None):
+        wait = shard_copy(FIRST, p, part, origin, core, targets[FIRST]).wait_recv
+        if valid is None:
+            wait()
+        else:
+            pl.when(valid)(wait)
 
     up, down = z < planes - 1, z > 0
-    lines = [(y, x), (ya, xa)]
-    far_lines = [(yb, xb), (1 - y, 1 - x)]
+
+    def both_ways(k):
+        if k == 0:
+            return [(z, None, None)]
+        return [(z - k, z - k >= 0, 1), (z + k, z + k < planes, -1)]
+
+    def begin(p):
+        for copy in own[p]:
+            copy.wait()
+        mine = chip(y, z, x)
+        for part in range(2):
+            send(UP, p, part, mine, up)
+            send(DOWN, p, part, mine, down)
+            send(FIRST, p, part, mine)
+        for part in range(2):
+            send(LAST, p, part, mine)
+            send(CORE, p, part, mine)
 
     def step(p, k):
         if k == 0:
-            own[p].wait()
-            mine = chip(y, z, x)
-            for way, cond in ((1, up), (2, down), (0, None), (3, None), (4, None)):
-                send(way, p, mine, cond)
             other = chip(ya, z, xa)
-            arrive(p, other)
-            for way, cond in ((1, up), (2, down), (3, None), (4, None)):
-                send(way, p, other, cond)
+            arrive(p, 0, other)
+            send(UP, p, 0, other, up)
+            send(DOWN, p, 0, other, down)
+            send(LAST, p, 0, other)
+            send(CORE, p, 0, other)
             return
-        for yy, xx in lines:
-            for sign, way in ((-1, 1), (1, 2)):
-                zz = z + sign * k
-                valid = (zz >= 0) if sign < 0 else (zz < planes)
-                onward = jnp.logical_and(valid, up if way == 1 else down)
+        for part, (yy, xx) in ((0, (y, x)), (1, (y, x)), (0, (ya, xa))):
+            for zz, valid, sign in both_ways(k):
                 origin = chip(yy, zz, xx)
-                pl.when(valid)(functools.partial(arrive, p, origin))
-                send(way, p, origin, onward)
-                send(3, p, origin, valid)
-                send(4, p, origin, valid)
+                arrive(p, part, origin, valid)
+                if sign == 1:
+                    send(UP, p, part, origin, jnp.logical_and(valid, up))
+                else:
+                    send(DOWN, p, part, origin, jnp.logical_and(valid, down))
+                if part == 1:
+                    send(FIRST, p, part, origin, valid)
+                send(LAST, p, part, origin, valid)
+                send(CORE, p, part, origin, valid)
 
     def across(p, k):
-        for yy, xx in far_lines:
-            for sign in (-1, 1) if k else (0,):
-                zz = z + sign * k
-                valid = jnp.logical_and(zz >= 0, zz < planes)
+        for zz, valid, _ in both_ways(k):
+            origin = chip(ya, zz, xa)
+            arrive(p, 1, origin, valid)
+            send(LAST, p, 1, origin, valid)
+            send(CORE, p, 1, origin, valid)
+        for part, (yy, xx) in ((0, (yb, xb)), (1, (yb, xb)), (0, (1 - y, 1 - x))):
+            for zz, valid, _ in both_ways(k):
                 origin = chip(yy, zz, xx)
-                pl.when(valid)(functools.partial(arrive, p, origin))
-                send(4, p, origin, valid)
-
-    def from_core(p):
-        for origin in range(devices // CORES):
-            pltpu.make_async_remote_copy(
-                src_ref=wbuf.at[p, origin * CORES + 1 - core],
-                dst_ref=wbuf.at[p, origin * CORES + 1 - core],
-                send_sem=send_sem.at[4, p, origin],
-                recv_sem=recv_sem.at[1, p, origin],
-                device_id=targets[4],
-                device_id_type=MESH,
-            ).wait_recv()
+                arrive(p, part, origin, valid)
+                send(CORE, p, part, origin, valid)
+
+    def settle(p, k):
+        for zz, valid, _ in both_ways(k):
+            origin = chip(1 - y, zz, 1 - x)
+            arrive(p, 1, origin, valid)
+            send(CORE, p, 1, origin, valid)
+        for zz, valid, _ in both_ways(k):
+
+            def finish():
+                for yy in range(2):
+                    for xx in range(WIDE):
+                        for part in range(2):
+                            shard_copy(
+                                CORE, p, part, chip(yy, zz, xx), 1 - core, targets[CORE]
+                            ).wait_recv()
+                project(p, zz, k == 0)
+
+            if valid is None:
+                finish()
+            else:
+                pl.when(valid)(finish)
+
+    def project(p, zz, first):
+        if first:
+            (x_load, g_load)[p].wait()
+        terms = []
+        for yy in range(2):
+            base = (yy * planes + zz) * WIDE * CORES
+            cols = pl.ds(pl.multiple_of(base * rows, 128), WIDE * CORES * rows)
+            block = wbuf[p, pl.ds(base, WIDE * CORES)].reshape(WIDE * CORES * rows, 2 * head)
+            if p == 0:
+                terms.append(jnp.dot(xv[:, cols], block, preferred_element_type=jnp.float32))
+            else:
+                terms.append(
+                    jnp.concatenate(
+                        [
+                            jnp.dot(
+                                xv[:, cols], block[:, :head], preferred_element_type=jnp.float32
+                            ),
+                            jnp.dot(
+                                gv[:, cols], block[:, head:], preferred_element_type=jnp.float32
+                            ),
+                        ],
+                        axis=-1,
+                    )
+                )
+        total = terms[0] + terms[1]
+        proj[p] = total if first else proj[p] + total
 
     parts = 4 if devices % 4 == 0 else 1
     group = devices // parts
@@ -208,17 +282,6 @@
     def weights(p, i, low, high):
         block = wbuf[p, i * group : (i + 1) * group]
         return block.reshape(span, 2 * head)[:, low:high]
-
-    def project(ref, p, low, high):
-        total = None
-        for i in range(parts):
-            term = jnp.dot(
-                ref[:, i * span : (i + 1) * span],
-                weights(p, i, low, high),
-                preferred_element_type=jnp.float32,
-            )
-            total = term if total is None else total + term
-        return total
 
     place = x * CORES + core
     state_waits = []
@@ -286,38 +349,34 @@
                     dst_ref=sum_in.at[e, dz - 1],
                     send_sem=sum_ss.at[e, dz - 1],
                     recv_sem=sum_rs.at[e, dz - 1],
-                    device_id=targets[4],
+                    device_id=targets[CORE],
                     device_id_type=MESH,
                 ).wait_recv()
                 acc[...] += sum_in[e, dz - 1].astype(jnp.float32)
 
         return acc[...].astype(jnp.bfloat16)
 
-    for k in range(planes):
-        step(0, k)
-        if k >= 1:
-            across(0, k - 1)
-            step(1, k - 1)
-        if k >= 2:
-            across(1, k - 2)
-    across(0, planes - 1)
-    step(1, planes - 1)
-    if planes >= 2:
-        across(1, planes - 2)
-    from_core(0)
-
-    x_load.wait()
-    kv = project(xv, 0, 0, 2 * head).astype(jnp.bfloat16)
-    key_rows, value_rows = kv[:, :head], kv[:, head:]
-    local_state = contract(key_rows, value_rows, 0, 0)
-    spread(0, local_state)
-    across(1, planes - 1)
-    plane_sum(0, local_state)
-    from_core(1)
-
-    queries = project(xv, 1, 0, head).astype(jnp.bfloat16)
-    g_load.wait()
-    head_grad = project(gv, 1, head, 2 * head)
+    for p in range(PIECES):
+        begin(p)
+    order = [(p, k) for k in range(planes) for p in range(PIECES)]
+    keyval_at = order.index((0, planes - 1)) + 2
+    for i in range(len(order) + 2):
+        if i < len(order):
+            step(*order[i])
+        if 1 <= i <= len(order):
+            across(*order[i - 1])
+        if i == keyval_at + 1:
+            plane_sum(0, local_state)
+        if i >= 2:
+            settle(*order[i - 2])
+        if i == keyval_at:
+            kv = proj[0].astype(jnp.bfloat16)
+            key_rows, value_rows = kv[:, :head], kv[:, head:]
+            local_state = contract(key_rows, value_rows, 0, 0)
+            spread(0, local_state)
+
+    queries = proj[1, :, :head].astype(jnp.bfloat16)
+    head_grad = proj[1, :, head:]
     row_ids = lax.broadcasted_iota(jnp.int32, (count, count), 0)
     col_ids = lax.broadcasted_iota(jnp.int32, (count, count), 1)
     causal = row_ids >= col_ids
@@ -341,6 +400,10 @@
     plane_sum(1, local_grad)
     key_part = contract(prob_grad, queries, 0, 0)
     value_part = contract(scores, attn_grad, 0, 0)
+    for i in range(parts):
+        query_out[:, i * span : (i + 1) * span] = contract(
+            query_grad, weights(1, i, 0, head), 1, 1
+        )
     later_state = collect(1)
     key_grad = key_part + contract(value_rows, later_state, 1, 1)
     value_grad = value_part + jnp.dot(key_rows, later_state, preferred_element_type=jnp.float32)
@@ -350,7 +413,7 @@
         cols = pl.ds(i * span, span)
         ob[:, i * span : (i + 1) * span] = (
             contract(joined, weights(0, i, 0, 2 * head), 1, 1)
-            + contract(query_grad, weights(1, i, 0, head), 1, 1)
+            + query_out[:, i * span : (i + 1) * span]
         ).astype(jnp.bfloat16)
         copy = pltpu.make_async_copy(ob.at[:, cols], out_hbm.at[:, cols], out_sem.at[i])
         copy.start()
@@ -368,9 +431,6 @@
     tokens, grads_in = inputs[0], out_grad[0]
     count, width = tokens.shape
     rows, _, head = w_project.shape
-    keyval = w_project[:, 1:, :].reshape(rows, 2 * head)
-    other = jnp.concatenate([w_project[:, 0, :], w_output], axis=-1)
-    packed = jnp.stack([keyval, other])
     bf16, f32 = jnp.bfloat16, jnp.float32
     chips = devices // CORES
     hops = max(planes - 1, 1)
@@ -379,32 +439,34 @@
     result = pl.pallas_call(
         functools.partial(fused_kernel, planes),
         out_shape=jax.ShapeDtypeStruct((count, width), bf16),
-        in_specs=[any_spec, any_spec, any_spec, pl.BlockSpec(memory_space=pltpu.VMEM)],
+        in_specs=[pl.BlockSpec(memory_space=pltpu.HBM)] * 4 + [pl.BlockSpec(memory_space=pltpu.VMEM)],
         out_specs=any_spec,
         scratch_shapes=[
             pltpu.VMEM((count, width), bf16),
             pltpu.VMEM((count, width), bf16),
             pltpu.VMEM((PIECES, devices, rows, 2 * head), bf16),
             pltpu.VMEM((count, width), bf16),
+            pltpu.VMEM((PIECES, count, 2 * head), f32),
+            pltpu.VMEM((count, width), f32),
             pltpu.VMEM((2, head, head), bf16),
             pltpu.VMEM((2, 4, head, head), bf16),
             pltpu.VMEM((2, head, head), bf16),
             pltpu.VMEM((2, hops, head, head), bf16),
             pltpu.VMEM((head, head), f32),
             dma((2,)),
-            dma((PIECES,)),
             dma((4,)),
-            dma((2, PIECES, chips)),
-            dma((5, PIECES, chips)),
+            dma((4,)),
+            dma((2, PIECES, 2, chips)),
+            dma((5, PIECES, 2, chips)),
             dma((2, 4)),
             dma((2, 4)),
             dma((2, hops)),
             dma((2, hops)),
         ],
         compiler_params=pltpu.CompilerParams(
-            collective_id=0, has_side_effects=True, vmem_limit_bytes=48 * 1024 * 1024
+            collective_id=0, has_side_effects=True, vmem_limit_bytes=67043328
         ),
-    )(tokens, grads_in, packed, norm_gain.reshape(1, head))
+    )(tokens, grads_in, jnp.transpose(w_project, (1, 0, 2)), w_output, norm_gain.reshape(1, head))
     return result[None]
 
 

time: 66.4 us -> 62 us (0.934)
  local copies, waits for them, and re-layouts: 6.59 us -> 2.76 us
  other arithmetic: 0.83 us -> 0 us
    unnamed x7 -> x1, local copies, waits for them, and re-layouts: 4.71 us -> 2.76 us
    slice x2 -> x0, local copies, waits for them, and re-layouts: 1.01 us -> none  [per_device_fused(): keyval = w_project[:, 1:, :].reshape(rows, 2 * head)]
    another operation x2 -> x0, other arithmetic: 0.83 us -> none  [per_device_fused(): packed = jnp.stack([keyval, other])]
    squeeze x1 -> x0, local copies, waits for them, and re-layouts: 0.8 us -> none  [per_device_fused(): other = jnp.concatenate([w_project[:, 0, :], w_output], axis=-1)]
where the time goes in v2:
time: 62 us; the launch traced here: 61.9 us
  Pallas kernels  59.1 us (95%)
  local copies, waits for them, and re-layouts  2.76 us (4%)
    pallas_call x1, Pallas kernels, per_device_fused(): pl.pallas_call(functools.partial(fused_kernel, planes), out_shape=jax.Sha...  59.1 us
    unnamed x1, local copies, waits for them, and re-layouts  2.76 us

profile of v2, /device:TPU:0, one launch (start us, length us, event | category | flops | bytes accessed | tf_op | source)
XLA Modules:
  0.0 61.9 jit_solution(8937301532411455038)
XLA Ops:
  0.0 59.1 %shard_map.55 = bf16[136,6144]{1,0:T(8,128)(2,1)} custom-call(bf16[136,6144]{1,0:T(8,128)(2,1)} %bitcast.6, bf16[136,6144]{1,0:T(8,128)(2,1)} %bitcast.7, bf16[3,192,128]{2,1,0:T(8,128)(2,1)} %bitcast.8, bf16[192,128]{1,0:T(8,128)(2,1)} %o_hbm.1, f32[1,128]{1,0:T(1,128)} %bitcast.9), custom_call_target="tpu_custom_call" | custom-call | tf_op jit(solution)/shard_map/pallas_call | solution.py:439
  59.1 2.8 %copy.7 = bf16[1,136,6144]{2,1,0:T(8,128)(2,1)} copy(bf16[1,136,6144]{2,1,0:T(8,128)(2,1)} %bitcast.5) | data formatting | bytes 3342336

commit v3 on v2

--- a/solution.py
+++ b/solution.py
@@ -75,6 +75,8 @@
 CORES = 2
 WIDE = 2
 PIECES = 2
+ROUTED = 1
+PARTS = 1
 MESH = pl.DeviceIdType.MESH
 FIRST, UP, DOWN, LAST, CORE = range(5)
 
@@ -136,8 +138,7 @@
         pl.semaphore_signal(barrier, inc=1, device_id=other, device_id_type=MESH)
     pl.semaphore_wait(barrier, len(near))
 
-    cut = rows * 2 // 3 // 16 * 16
-    spans = (pl.ds(0, cut), pl.ds(cut, rows - cut))
+    spans = (pl.ds(0, rows),)
 
     def shard_copy(way, p, part, origin, owner, target):
         slot = wbuf.at[p, origin * CORES + owner, spans[part]]
@@ -185,24 +186,27 @@
         for copy in own[p]:
             copy.wait()
         mine = chip(y, z, x)
-        for part in range(2):
+        for part in range(PARTS):
             send(UP, p, part, mine, up)
             send(DOWN, p, part, mine, down)
             send(FIRST, p, part, mine)
-        for part in range(2):
+        for part in range(PARTS):
             send(LAST, p, part, mine)
             send(CORE, p, part, mine)
 
     def step(p, k):
         if k == 0:
             other = chip(ya, z, xa)
-            arrive(p, 0, other)
-            send(UP, p, 0, other, up)
-            send(DOWN, p, 0, other, down)
-            send(LAST, p, 0, other)
-            send(CORE, p, 0, other)
+            for part in range(ROUTED):
+                arrive(p, part, other)
+                send(UP, p, part, other, up)
+                send(DOWN, p, part, other, down)
+                send(LAST, p, part, other)
+                send(CORE, p, part, other)
             return
-        for part, (yy, xx) in ((0, (y, x)), (1, (y, x)), (0, (ya, xa))):
+        for part, (yy, xx) in [(part, (y, x)) for part in range(PARTS)] + [
+            (part, (ya, xa)) for part in range(ROUTED)
+        ]:
             for zz, valid, sign in both_ways(k):
                 origin = chip(yy, zz, xx)
                 arrive(p, part, origin, valid)
@@ -210,18 +214,15 @@
                     send(UP, p, part, origin, jnp.logical_and(valid, up))
                 else:
                     send(DOWN, p, part, origin, jnp.logical_and(valid, down))
-                if part == 1:
+                if part >= ROUTED:
                     send(FIRST, p, part, origin, valid)
                 send(LAST, p, part, origin, valid)
                 send(CORE, p, part, origin, valid)
 
     def across(p, k):
-        for zz, valid, _ in both_ways(k):
-            origin = chip(ya, zz, xa)
-            arrive(p, 1, origin, valid)
-            send(LAST, p, 1, origin, valid)
-            send(CORE, p, 1, origin, valid)
-        for part, (yy, xx) in ((0, (yb, xb)), (1, (yb, xb)), (0, (1 - y, 1 - x))):
+        for part, (yy, xx) in [(part, (yb, xb)) for part in range(PARTS)] + [
+            (part, (1 - y, 1 - x)) for part in range(ROUTED)
+        ]:
             for zz, valid, _ in both_ways(k):
                 origin = chip(yy, zz, xx)
                 arrive(p, part, origin, valid)
@@ -229,15 +230,11 @@
 
     def settle(p, k):
         for zz, valid, _ in both_ways(k):
-            origin = chip(1 - y, zz, 1 - x)
-            arrive(p, 1, origin, valid)
-            send(CORE, p, 1, origin, valid)
-        for zz, valid, _ in both_ways(k):
 
             def finish():
                 for yy in range(2):
                     for xx in range(WIDE):
-                        for part in range(2):
+                        for part in range(PARTS):
                             shard_copy(
                                 CORE, p, part, chip(yy, zz, xx), 1 - core, targets[CORE]
                             ).wait_recv()
@@ -291,7 +288,7 @@
 
     def spread(e, local):
         st_send[e] = local.astype(jnp.bfloat16)
-        for j in range(1, 4):
+        for j in (2, 3, 1):
             px, pc = plane_peer(j)
             copy = pltpu.make_async_remote_copy(
                 src_ref=st_send.at[e],
@@ -324,7 +321,7 @@
             partial = partial + jnp.where(chosen, block, 0.0)
         acc[...] = partial
         sum_send[e] = total.astype(jnp.bfloat16)
-        for dz in range(1, planes):
+        for dz in range(planes - 1, 0, -1):
             zz = z + dz if e == 0 else z - dz
             valid = (zz < planes) if e == 0 else (zz >= 0)
             copy = pltpu.make_async_remote_copy(
@@ -456,8 +453,8 @@
             dma((2,)),
             dma((4,)),
             dma((4,)),
-            dma((2, PIECES, 2, chips)),
-            dma((5, PIECES, 2, chips)),
+            dma((2, PIECES, PARTS, chips)),
+            dma((5, PIECES, PARTS, chips)),
             dma((2, 4)),
             dma((2, 4)),
             dma((2, hops)),

time: 62 us -> 59.7 us (0.963)
  Pallas kernels: 59.1 us -> 56.8 us
    pallas_call x1, Pallas kernels: 59.1 us -> 56.8 us  [per_device_fused(): pl.pallas_call(functools.partial(fused_kernel, planes), out_shape=jax.Sha...]
where the time goes in v3:
time: 59.7 us; the launch traced here: 59.6 us
  Pallas kernels  56.8 us (95%)
  local copies, waits for them, and re-layouts  2.76 us (5%)
    pallas_call x1, Pallas kernels, per_device_fused(): pl.pallas_call(functools.partial(fused_kernel, planes), out_shape=jax.Sha...  56.8 us
    unnamed x1, local copies, waits for them, and re-layouts  2.76 us

profile of v3, /device:TPU:0, one launch (start us, length us, event | category | flops | bytes accessed | tf_op | source)
XLA Modules:
  0.0 59.6 jit_solution(4435007451085564294)
XLA Ops:
  0.0 56.8 %shard_map.55 = bf16[136,6144]{1,0:T(8,128)(2,1)} custom-call(bf16[136,6144]{1,0:T(8,128)(2,1)} %bitcast.6, bf16[136,6144]{1,0:T(8,128)(2,1)} %bitcast.7, bf16[3,192,128]{2,1,0:T(8,128)(2,1)} %bitcast.8, bf16[192,128]{1,0:T(8,128)(2,1)} %o_hbm.1, f32[1,128]{1,0:T(1,128)} %bitcast.9), custom_call_target="tpu_custom_call" | custom-call | tf_op jit(solution)/shard_map/pallas_call | solution.py:436
  56.8 2.8 %copy.7 = bf16[1,136,6144]{2,1,0:T(8,128)(2,1)} copy(bf16[1,136,6144]{2,1,0:T(8,128)(2,1)} %bitcast.5) | data formatting | bytes 3342336

commit v4 on v3

--- a/solution.py
+++ b/solution.py
@@ -355,7 +355,10 @@
 
     for p in range(PIECES):
         begin(p)
-    order = [(p, k) for k in range(planes) for p in range(PIECES)]
+    order = [(0, 0)]
+    for k in range(1, planes):
+        order += [(0, k), (1, k - 1)]
+    order.append((1, planes - 1))
     keyval_at = order.index((0, planes - 1)) + 2
     for i in range(len(order) + 2):
         if i < len(order):

time: 59.7 us -> 57.5 us (0.963)
  Pallas kernels: 56.8 us -> 54.6 us
    pallas_call x1, Pallas kernels: 56.8 us -> 54.6 us  [per_device_fused(): pl.pallas_call(functools.partial(fused_kernel, planes), out_shape=jax.Sha...]
where the time goes in v4:
time: 57.5 us; the launch traced here: 57.4 us
  Pallas kernels  54.6 us (95%)
  local copies, waits for them, and re-layouts  2.76 us (5%)
    pallas_call x1, Pallas kernels, per_device_fused(): pl.pallas_call(functools.partial(fused_kernel, planes), out_shape=jax.Sha...  54.6 us
    unnamed x1, local copies, waits for them, and re-layouts  2.76 us

profile of v4, /device:TPU:0, one launch (start us, length us, event | category | flops | bytes accessed | tf_op | source)
XLA Modules:
  0.0 57.4 jit_solution(2275128278603997124)
XLA Ops:
  0.0 54.6 %shard_map.55 = bf16[136,6144]{1,0:T(8,128)(2,1)} custom-call(bf16[136,6144]{1,0:T(8,128)(2,1)} %bitcast.6, bf16[136,6144]{1,0:T(8,128)(2,1)} %bitcast.7, bf16[3,192,128]{2,1,0:T(8,128)(2,1)} %bitcast.8, bf16[192,128]{1,0:T(8,128)(2,1)} %o_hbm.1, f32[1,128]{1,0:T(1,128)} %bitcast.9), custom_call_target="tpu_custom_call" | custom-call | tf_op jit(solution)/shard_map/pallas_call | solution.py:439
  54.6 2.8 %copy.7 = bf16[1,136,6144]{2,1,0:T(8,128)(2,1)} copy(bf16[1,136,6144]{2,1,0:T(8,128)(2,1)} %bitcast.5) | data formatting | bytes 3342336
